TPU v7x, 32 devices: a whole 2x2x4 slice. The times are simulated.
32 devices in a mesh: dp: 1, fsdp: 32 (over z, y, x, core).
Axes of the slice: x: 2, y: 2, z: 4, core: 2. Of those that a mesh axis runs over, the one named last changes fastest.
Arguments:
- hidden_states: bfloat16 [128, 4096], P(('dp', 'fsdp')), may hold values from -400 to 400
- token_ids: int32 [128], P(('dp', 'fsdp')), may hold values from 0 to 4095
- norm_gain: float32 [4096], replicated, may hold values from 0.5 to 1.5
- ref_gate_w: bfloat16 [4096, 14784], P('dp', 'fsdp'), may hold values from -0.1875 to 0.1875
- ref_up_w: bfloat16 [4096, 14784], P('dp', 'fsdp'), may hold values from -0.1875 to 0.1875
- ref_down_w: bfloat16 [14784, 4096], P('fsdp', 'dp'), may hold values from -0.09375 to 0.09375
- pol_gate_w: bfloat16 [4096, 14784], P('dp', 'fsdp'), may hold values from -0.1875 to 0.1875
- pol_up_w: bfloat16 [4096, 14784], P('dp', 'fsdp'), may hold values from -0.1875 to 0.1875
- pol_down_w: bfloat16 [14784, 4096], P('fsdp', 'dp'), may hold values from -0.09375 to 0.09375
- sample_lengths: int32 [1, 32], P('dp'), may hold values from 1 to 24, 128 in all within a row
- prompt_index: int32 [1, 32], P('dp'), may hold values from 0 to 3, as said below
- rewards: float32 [1, 32], P('dp'), may hold values from -6 to 6
Outputs:
- grad_gate: float32 [4096, 14784], P('dp', 'fsdp')
- grad_up: float32 [4096, 14784], P('dp', 'fsdp')
- grad_down: float32 [14784, 4096], P('fsdp', 'dp')
- advantage: float32 [1, 32], P('dp')
Inputs may be any that keep to these rules, and one draw needn't show every extreme that they name: `prompt_index`: in each row, every prompt from 0 to 3 is answered by exactly 8 samples. `sample_lengths`: each row sums to 128.
All inputs are finite; a program needn't handle non-finite values.
Results may differ from a plain program's by a relative error of at most 0.013.
Values may be sent and summed in bfloat16 or wider, within the bound.
No kernel may reach another device: no remote copies, remote signals or barrier semaphores. Data moves between devices by JAX's collectives and lax.ppermute only.
A program may use at most 128 MiB of HBM per device.

v0:
```python
import jax
import jax.numpy as jnp
from jax import lax
from jax.sharding import PartitionSpec as P

K = 8
EPSILON = 1e-06
KL_WEIGHT = 0.05


def combined_all(part, axis, combine):
    gathered = jax.tree.map(lambda a: lax.all_gather(a, axis), part)

    def take(source):
        return jax.tree.map(lambda a: lax.dynamic_index_in_dim(a, source, 0, False), gathered)

    return lax.fori_loop(
        1, lax.axis_size(axis), lambda source, state: combine(state, take(source)), take(0)
    )


def normalize(states, norm_gain):
    values = states.astype(jnp.float32)
    factor = lax.rsqrt(jnp.mean(values * values, axis=-1, keepdims=True) + EPSILON)
    return (values * factor * norm_gain).astype(jnp.bfloat16)


def combine_totals(first, second):
    row_peak = jnp.maximum(first[0], second[0])
    summed = first[1] * jnp.exp(first[0] - row_peak) + second[1] * jnp.exp(second[0] - row_peak)
    return (row_peak, summed, first[2] + second[2])


def column_section(normed_cols, state_cols, ids_all, weight_sets, group_index):
    col_width = state_cols.shape[1]
    unit_count = weight_sets[0][0].shape[1]
    in_weights = jnp.concatenate(
        [matrix for triple in weight_sets for matrix in triple[:2]], axis=1
    )
    row_block = normed_cols
    pre_sums = lax.psum_scatter(
        jnp.dot(row_block, in_weights, preferred_element_type=jnp.float32),
        "dp",
        scatter_dimension=0,
        tiled=True,
    )
    gate_pre = pre_sums[:, 0:unit_count]
    up_pre = pre_sums[:, unit_count : 2 * unit_count]
    activations = jax.nn.silu(gate_pre) * up_pre
    hidden_local = activations.astype(jnp.bfloat16)
    hidden_all = lax.all_gather(hidden_local, "dp", axis=0, tiled=True)
    row_block = hidden_all
    pieces = jnp.dot(row_block, weight_sets[0][2], preferred_element_type=jnp.float32)
    out_cols = lax.psum_scatter(pieces, "fsdp", scatter_dimension=0, tiled=True)
    states = state_cols.astype(jnp.float32)
    col_ids = jnp.arange(col_width, dtype=jnp.int32) + group_index * col_width
    logits = states + out_cols
    row_peak = jnp.max(logits, axis=1)
    logits_list = [logits]
    peaks = [row_peak]
    sums = [jnp.sum(jnp.exp(logits - row_peak[:, None]), axis=1)]
    picks = [jnp.sum(jnp.where(col_ids[None, :] == ids_all[:, None], logits, 0.0), axis=1)]
    row_peak, summed, picked = combined_all(
        (jnp.stack(peaks, axis=1), jnp.stack(sums, axis=1), jnp.stack(picks, axis=1)),
        "dp",
        combine_totals,
    )
    log_total = row_peak + jnp.log(summed)
    return (pre_sums, hidden_all, logits_list, log_total, picked - log_total)


def leave_one_out(log_gap, inside, prompt_index, rewards):
    divergence = lax.psum(jnp.sum(log_gap[:, None] * inside, axis=0), "fsdp")
    scores = rewards[0] - KL_WEIGHT * divergence
    same_prompt = (prompt_index[0][:, None] == prompt_index[0][None, :]).astype(jnp.float32)
    others = jnp.sum(same_prompt * scores[None, :], axis=1) - scores
    advantage = scores - others / (K - 1)
    weight = jnp.sum(inside * advantage[None, :], axis=1)
    return (advantage, weight)


def local(
    hidden_states,
    token_ids,
    norm_gain,
    ref_gate_w,
    ref_up_w,
    ref_down_w,
    pol_gate_w,
    pol_up_w,
    pol_down_w,
    sample_lengths,
    prompt_index,
    rewards,
):
    token_count = hidden_states.shape[0]
    model_width = hidden_states.shape[1]
    group_index = lax.axis_index("dp")
    member_index = lax.axis_index("fsdp")
    unit_count = pol_gate_w.shape[1]
    normed = normalize(hidden_states, norm_gain)
    normed_mixed, state_cols = (
        lax.all_to_all(normed, "dp", split_axis=1, concat_axis=0, tiled=True),
        lax.all_to_all(hidden_states, "dp", split_axis=1, concat_axis=0, tiled=True),
    )
    normed_cols = lax.all_gather(normed_mixed, "fsdp", axis=0, tiled=True)
    ids_all = lax.all_gather(token_ids, "dp", axis=0, tiled=True)
    own_start = group_index * token_count
    position = member_index * token_count + jnp.arange(token_count, dtype=jnp.int32)
    sample_ends = jnp.cumsum(sample_lengths[0])
    sample_starts = sample_ends - sample_lengths[0]
    inside = (
        (position[:, None] >= sample_starts[None, :]) & (position[:, None] < sample_ends[None, :])
    ).astype(jnp.float32)
    _, _, _, _, ref_lp = column_section(
        normed_cols, state_cols, ids_all, [(ref_gate_w, ref_up_w, ref_down_w)], group_index
    )
    ref_own = lax.dynamic_slice_in_dim(ref_lp[:, 0], own_start, token_count, 0)
    group_normed = lax.all_gather(normed, "fsdp", axis=0, tiled=True)
    row_block = group_normed
    gate_pre = jnp.dot(
        row_block,
        lax.all_gather(pol_gate_w, "dp", axis=0, tiled=True),
        preferred_element_type=jnp.float32,
    )
    up_pre = jnp.dot(
        row_block,
        lax.all_gather(pol_up_w, "dp", axis=0, tiled=True),
        preferred_element_type=jnp.float32,
    )
    down_full = lax.all_gather(pol_down_w, "dp", axis=1, tiled=True)
    hidden = (jax.nn.silu(gate_pre) * up_pre).astype(jnp.bfloat16)
    row_block = hidden
    pol_out = lax.psum_scatter(
        jnp.dot(row_block, down_full, preferred_element_type=jnp.float32),
        "fsdp",
        scatter_dimension=0,
        tiled=True,
    )
    logits = hidden_states.astype(jnp.float32) + pol_out
    row_peak = jnp.max(logits, axis=1)
    log_total = row_peak + jnp.log(jnp.sum(jnp.exp(logits - row_peak[:, None]), axis=1))
    columns = jnp.arange(model_width, dtype=jnp.int32)
    onehot = (columns[None, :] == token_ids[:, None]).astype(jnp.float32)
    pol_own = (
        jnp.sum(jnp.where(columns[None, :] == token_ids[:, None], logits, 0.0), axis=1) - log_total
    )
    advantage, weight = leave_one_out(pol_own - ref_own, inside, prompt_index, rewards)
    grad_logits = (-weight[:, None] * (onehot - jnp.exp(logits - log_total[:, None]))).astype(
        jnp.bfloat16
    )
    group_grads = lax.all_gather(grad_logits, "fsdp", axis=0, tiled=True)
    down_term = lax.dot_general(
        hidden, group_grads, (((0,), (0,)), ((), ())), preferred_element_type=jnp.float32
    )
    grad_down = lax.psum_scatter(
        down_term.astype(jnp.bfloat16), "dp", scatter_dimension=1, tiled=True
    ).astype(jnp.float32)
    grad_hidden = lax.dot_general(
        group_grads, down_full, (((1,), (1,)), ((), ())), preferred_element_type=jnp.float32
    )
    sigmoid_gate = jax.nn.sigmoid(gate_pre)
    grad_gate_pre = grad_hidden * up_pre * sigmoid_gate * (1.0 + gate_pre * (1.0 - sigmoid_gate))
    grad_up_pre = grad_hidden * gate_pre * sigmoid_gate
    gate_grads = jnp.concatenate(
        [grad_gate_pre.astype(jnp.bfloat16), grad_up_pre.astype(jnp.bfloat16)], axis=1
    )
    row_block = group_normed
    grad_inner = lax.psum_scatter(
        lax.dot_general(
            row_block, gate_grads, (((0,), (0,)), ((), ())), preferred_element_type=jnp.float32
        ).astype(jnp.bfloat16),
        "dp",
        scatter_dimension=0,
        tiled=True,
    ).astype(jnp.float32)
    return (grad_inner[:, :unit_count], grad_inner[:, unit_count:], grad_down, advantage[None, :])


def solution(mesh):
    return jax.shard_map(
        local,
        mesh=mesh,
        in_specs=(
            P(("dp", "fsdp"), None),
            P(("dp", "fsdp")),
            P(),
            P("dp", "fsdp"),
            P("dp", "fsdp"),
            P("fsdp", "dp"),
            P("dp", "fsdp"),
            P("dp", "fsdp"),
            P("fsdp", "dp"),
            P("dp", None),
            P("dp", None),
            P("dp", None),
        ),
        out_specs=(P("dp", "fsdp"), P("dp", "fsdp"), P("fsdp", "dp"), P("dp", None)),
        check_vma=False,
    )
```

profile of v0, /device:TPU:0, one launch (start us, length us, event | category | flops | bytes accessed | tf_op | source)
XLA Modules:
  0.0 356.7 jit_solution(6231580681784564363)
XLA Ops:
  7.2 0.0 all-gather.5.cloned.1.call-start
  7.2 0.9 fusion.12
  8.1 1.5 fusion.15
  9.6 0.0 all-reduce.5.cloned.1.call-start
  9.7 58.1 %all-gather.5.cloned.1.call-done = bf16[32,4,4096]{2,1,0:T(4,128)(2,1)} async-done(((bf16[1,4,4096]{2,1,0:T(4,128)(2,1)}), bf16[32,4,4096]{2,1,0:T(4,128)(2,1)}) %all-gather.5.cloned.1.call-update) | async-done | bytes 1048592 | tf_op jit(solution)/shard_map/all_gather | solution.py:119
  67.8 1.3 reshape.84
  69.1 3.4 fusion.24
  72.5 1.2 multiply_convert_fusion.2
  73.7 0.9 copy-done
  74.6 2.1 fusion.25
  76.7 1.1 copy-done.8
  77.8 2.1 fusion
  80.0 2.1 fusion.9
  82.1 0.0 all-gather.7.cloned.1.call-start
  82.2 0.1 copy.19
  82.3 0.1 reduce-window.4
  82.3 0.1 reduce
  82.5 141.3 %all-reduce.5.cloned.1.call-done = (f32[128,4096]{1,0:T(8,128)}, f32[128,4096]{1,0:T(8,128)}) async-done(((f32[128,4096]{1,0:T(8,128)}, f32[128,4096]{1,0:T(8,128)}), (f32[128,4096]{1,0:T(8,128)}, f32[128,4096]{1,0:T(8,128)})) %all-reduce.5.cloned.1.call-update) | async-done | bytes 4194320
  223.8 1.1 fusion.17
  224.8 1.2 exponential_reduce_fusion
  226.1 1.1 exponential_reduce_fusion.1
  227.2 0.1 select_reduce_fusion.4
  227.3 39.5 %psum.7 = f32[32]{0:T(128)S(1)} all-reduce(f32[32]{0:T(128)S(1)} %get-tuple-element.12), channel_id=1, replica_groups=mesh['dp'=1,'fsdp'=32] {'fsdp'}, use_global_device_ids=true, to_apply=%region_11.12 | all-reduce | flops 32 | bytes 256 | tf_op jit(solution)/shard_map/psum | solution.py:73
  266.9 0.2 select_reduce_fusion.2
  267.1 0.1 select_reduce_fusion.3
  267.2 1.6 fusion.16
  268.8 53.2 %all-gather.7.cloned.1.call-done = bf16[32,4,4096]{2,1,0:T(4,128)(2,1)} async-done(((bf16[1,4,4096]{2,1,0:T(4,128)(2,1)}), bf16[32,4,4096]{2,1,0:T(4,128)(2,1)}) %all-gather.7.cloned.1.call-update) | async-done | bytes 1048592 | tf_op jit(solution)/shard_map/all_gather | solution.py:152
  322.1 1.3 reshape.86
  323.4 4.3 %fusion.4 = f32[462,4096]{1,0:T(8,128)} fusion(bf16[128,462]{0,1:T(8,128)(2,1)S(1)} %get-tuple-element.20, bf16[128,4096]{1,0:T(8,128)(2,1)S(1)} %reshape.86), kind=kOutput, calls=%fused_computation.6 | convolution fusion | flops 488226816 | bytes 8736256 | tf_op jit(solution)/shard_map/dot_general | solution.py:153
  327.7 1.1 multiply_convert_fusion.1
  328.8 7.5 %convert_convert_fusion = f32[4096,924]{0,1:T(8,128)} fusion(bf16[128,4096]{1,0:T(8,128)(2,1)S(1)} %reshape.84, bf16[128,462]{0,1:T(8,128)(2,1)S(1)} %get-tuple-element.19, bf16[128,462]{0,1:T(8,128)(2,1)S(1)} %get-tuple-element.18), kind=kOutput, calls=%fused_computation.4 | convolution fusion | flops 976926720 | bytes 16423936 | tf_op jit(solution)/shard_map/dot_general | solution.py:170
  336.3 13.9 %fusion.23 = (f32[4096,462]{0,1:T(8,128)}, f32[4096,462]{0,1:T(8,128)}) fusion(f32[4096,924]{0,1:T(8,128)} %convert_convert_fusion), kind=kLoop, calls=%fused_computation.50 | loop fusion | bytes 30277632 | tf_op jit(solution)/shard_map/slice | solution.py:177
  (32 shorter events, 0.2 us)
Async XLA Ops:
  7.2 60.6 %all-gather.5.cloned.1.call-start = ((), (), s32[]{:S(2)}) async-start(), calls=%async_computation | async-start | bytes 1081344 | tf_op jit(solution)/shard_map/all_gather | solution.py:119
  9.6 214.1 %all-reduce.5.cloned.1.call-start = ((), (), s32[]{:S(2)}) async-start(), calls=%async_computation.2 | async-start | bytes 8388608
  69.1 3.4 copy-start.2
  72.5 2.1 copy-start
  72.5 4.1 %copy-start.9 = (bf16[4096,462]{0,1:T(8,128)(2,1)S(1)}, bf16[4096,462]{0,1:T(8,128)(2,1)}, u32[]{:S(2)}) copy-start(bf16[4096,462]{0,1:T(8,128)(2,1)} %param.15) | copy-start | bytes 11354116
  73.7 4.1 %copy-start.8 = (bf16[4096,462]{0,1:T(8,128)(2,1)S(1)}, bf16[4096,462]{0,1:T(8,128)(2,1)}, u32[]{:S(2)}) copy-start(bf16[4096,462]{0,1:T(8,128)(2,1)} %param.16) | copy-start | bytes 11354116
  77.8 2.1 copy-start.3
  79.9 2.2 copy-start.7
  80.0 143.8 %copy-start.4 = (bf16[4,4096]{1,0:T(4,128)(2,1)S(1)}, bf16[4,4096]{1,0:T(4,128)(2,1)}, u32[]{:S(2)}) copy-start(bf16[4,4096]{1,0:T(4,128)(2,1)} %param.12) | copy-start | bytes 98308
  80.0 144.8 %copy-start.5 = (s32[4]{0:T(128)S(1)}, s32[4]{0:T(128)}, u32[]{:S(2)}) copy-start(s32[4]{0:T(128)} %param.13) | copy-start | bytes 52
  82.1 184.8 %copy-start.10 = (f32[1,32]{1,0:T(1,128)S(1)}, f32[1,32]{1,0:T(1,128)}, u32[]{:S(2)}) copy-start(f32[1,32]{1,0:T(1,128)} %param.23) | copy-start | bytes 388
  82.1 184.8 %copy-start.6 = (s32[1,32]{1,0:T(1,128)S(1)}, s32[1,32]{1,0:T(1,128)}, u32[]{:S(2)}) copy-start(s32[1,32]{1,0:T(1,128)} %param.22) | copy-start | bytes 388
  82.1 239.9 %all-gather.7.cloned.1.call-start = ((), (), s32[]{:S(2)}) async-start(), calls=%async_computation.1 | async-start | bytes 1081344 | tf_op jit(solution)/shard_map/all_gather | solution.py:152
  267.0 60.6 %copy-start.11 = (f32[32]{0:T(128)}, f32[32]{0:T(128)S(1)}, u32[]{:S(2)}) copy-start(f32[32]{0:T(128)S(1)} %multiply_subtract_fusion) | copy-start | bytes 388
  323.4 4.3 %copy-start.1 = (bf16[462,4096]{1,0:T(8,128)(2,1)S(1)}, bf16[462,4096]{1,0:T(8,128)(2,1)}, u32[]{:S(2)}) copy-start(bf16[462,4096]{1,0:T(8,128)(2,1)} %param.20) | copy-start | bytes 11354116
Sparse Core Ops, SparseCore 0:
  11.4 56.3 all-gather.4
  82.2 141.4 all-reduce.4
  269.0 53.0 all-gather.6
where the time goes:
time: 357 us
  waiting for transfers between devices  253 us (71%)
  blocking collectives  39.5 us (11%)
  matrix products  23.7 us (7%)
  local copies, waits for them, and re-layouts  18.7 us (5%)
  between operations  13.9 us (4%)
  other arithmetic  8.04 us (2%)
    unnamed x4, waiting for transfers between devices  141 us
    all_gather x1, waiting for transfers between devices, local(): group_normed = lax.all_gather(normed, 'fsdp', axis=0, tiled=True)  58.1 us
    all_gather x1, waiting for transfers between devices, local(): group_grads = lax.all_gather(grad_logits, 'fsdp', axis=0, tiled=True)  53.2 us
    psum x1, blocking collectives, leave_one_out(): divergence = lax.psum(jnp.sum(log_gap[:, None] * inside, axis=0), 'fsdp')  39.5 us
    slice x1, local copies, waits for them, and re-layouts, local(): grad_inner[:, unit_count:]  13.9 us
    dot_general x1, matrix products, local(): lax.dot_general(row_block, gate_grads, (((0,), (0,)), ((), ())), preferre...  7.46 us
  transfers between devices with their start and end apart: 3, of which 3 were waited for; matrix products, arithmetic and copies ran while one was open for 0% of the time, Pallas kernels for 0%

commit v1 on v0

--- a/solution.py
+++ b/solution.py
@@ -70,7 +70,7 @@
 
 
 def leave_one_out(log_gap, inside, prompt_index, rewards):
-    divergence = lax.psum(jnp.sum(log_gap[:, None] * inside, axis=0), "fsdp")
+    divergence = jnp.sum(lax.all_gather(jnp.sum(log_gap[:, None] * inside, axis=0), "fsdp"), axis=0)
     scores = rewards[0] - KL_WEIGHT * divergence
     same_prompt = (prompt_index[0][:, None] == prompt_index[0][None, :]).astype(jnp.float32)
     others = jnp.sum(same_prompt * scores[None, :], axis=1) - scores

time: 357 us -> 358 us (level)
    psum x1 -> x0, blocking collectives: 39.5 us -> none  [leave_one_out(): divergence = lax.psum(jnp.sum(log_gap[:, None] * inside, axis=0), 'fsdp')]
    unnamed x0 -> x1, blocking collectives: none -> 39.5 us
where the time goes in v1:
time: 358 us; the launch traced here: 357 us
  waiting for transfers between devices  253 us (71%)
  blocking collectives  39.5 us (11%)
  matrix products  23.7 us (7%)
  local copies, waits for them, and re-layouts  19 us (5%)
  between operations  14 us (4%)
  other arithmetic  8.06 us (2%)
    unnamed x4, waiting for transfers between devices  141 us
    all_gather x1, waiting for transfers between devices, local(): group_normed = lax.all_gather(normed, 'fsdp', axis=0, tiled=True)  58.1 us
    all_gather x1, waiting for transfers between devices, local(): group_grads = lax.all_gather(grad_logits, 'fsdp', axis=0, tiled=True)  53.2 us
    unnamed x1, blocking collectives  39.5 us
    slice x1, local copies, waits for them, and re-layouts, local(): grad_inner[:, unit_count:]  13.9 us
    dot_general x1, matrix products, local(): lax.dot_general(row_block, gate_grads, (((0,), (0,)), ((), ())), preferre...  7.46 us
  transfers between devices with their start and end apart: 3, of which 3 were waited for; matrix products, arithmetic and copies ran while one was open for 0% of the time, Pallas kernels for 0%

profile of v1, /device:TPU:0, one launch (start us, length us, event | category | flops | bytes accessed | tf_op | source)
XLA Modules:
  0.0 357.1 jit_solution(13420961613031663541)
XLA Ops:
  7.2 0.9 fusion.12
  8.1 1.5 fusion.15
  9.7 58.1 %all-gather.6.cloned.1.call-done = bf16[32,4,4096]{2,1,0:T(4,128)(2,1)} async-done(((bf16[1,4,4096]{2,1,0:T(4,128)(2,1)}), bf16[32,4,4096]{2,1,0:T(4,128)(2,1)}) %all-gather.6.cloned.1.call-update) | async-done | bytes 1048592 | tf_op jit(solution)/shard_map/all_gather | solution.py:119
  67.8 1.3 reshape.96
  69.1 3.4 fusion.27
  72.5 1.2 multiply_convert_fusion.2
  73.7 0.9 copy-done
  74.6 2.1 fusion.28
  76.7 1.1 copy-done.10
  77.8 2.1 fusion
  80.0 2.1 fusion.9
  82.1 0.0 all-gather.8.cloned.1.call-start
  82.2 0.1 copy.19
  82.3 0.1 reduce-window.4
  82.3 0.1 reduce
  82.5 141.3 %all-reduce.6.cloned.1.call-done = (f32[128,4096]{1,0:T(8,128)}, f32[128,4096]{1,0:T(8,128)}) async-done(((f32[128,4096]{1,0:T(8,128)}, f32[128,4096]{1,0:T(8,128)}), (f32[128,4096]{1,0:T(8,128)}, f32[128,4096]{1,0:T(8,128)})) %all-reduce.6.cloned.1.call-update) | async-done | bytes 4194320
  223.8 1.1 fusion.17
  224.9 1.2 exponential_reduce_fusion
  226.1 1.1 exponential_reduce_fusion.1
  227.3 0.1 select_reduce_fusion.4
  227.4 0.2 dynamic-update-slice
  227.6 39.5 %all-reduce = f32[1024]{0:T(1024)S(1)} all-reduce(f32[1024]{0:T(1024)S(1)} %dynamic-update-slice), channel_id=2, replica_groups=mesh['dp'=1,'fsdp'=32] {'fsdp'}, use_global_device_ids=true, to_apply=%add | all-reduce | flops 1024 | bytes 8192
  267.1 0.1 reshape.92
  267.2 0.2 select_reduce_fusion.2
  267.4 0.1 select_reduce_fusion.3
  267.6 1.6 fusion.16
  269.2 53.2 %all-gather.8.cloned.1.call-done = bf16[32,4,4096]{2,1,0:T(4,128)(2,1)} async-done(((bf16[1,4,4096]{2,1,0:T(4,128)(2,1)}), bf16[32,4,4096]{2,1,0:T(4,128)(2,1)}) %all-gather.8.cloned.1.call-update) | async-done | bytes 1048592 | tf_op jit(solution)/shard_map/all_gather | solution.py:152
  322.4 1.3 reshape.98
  323.8 4.3 %fusion.4 = f32[462,4096]{1,0:T(8,128)} fusion(bf16[128,462]{0,1:T(8,128)(2,1)S(1)} %get-tuple-element.20, bf16[128,4096]{1,0:T(8,128)(2,1)S(1)} %reshape.98), kind=kOutput, calls=%fused_computation.6 | convolution fusion | flops 488226816 | bytes 8736256 | tf_op jit(solution)/shard_map/dot_general | solution.py:153
  328.1 1.2 multiply_convert_fusion.1
  329.2 7.5 %convert_convert_fusion = f32[4096,924]{0,1:T(8,128)} fusion(bf16[128,4096]{1,0:T(8,128)(2,1)S(1)} %reshape.96, bf16[128,462]{0,1:T(8,128)(2,1)S(1)} %get-tuple-element.19, bf16[128,462]{0,1:T(8,128)(2,1)S(1)} %get-tuple-element.18), kind=kOutput, calls=%fused_computation.4 | convolution fusion | flops 976926720 | bytes 16423936 | tf_op jit(solution)/shard_map/dot_general | solution.py:170
  336.7 13.9 %fusion.26 = (f32[4096,462]{0,1:T(8,128)}, f32[4096,462]{0,1:T(8,128)}) fusion(f32[4096,924]{0,1:T(8,128)} %convert_convert_fusion), kind=kLoop, calls=%fused_computation.53 | loop fusion | bytes 30277632 | tf_op jit(solution)/shard_map/slice | solution.py:177
  (36 shorter events, 0.3 us)
Async XLA Ops:
  7.2 60.6 %all-gather.6.cloned.1.call-start = ((), (), s32[]{:S(2)}) async-start(), calls=%async_computation | async-start | bytes 1081344 | tf_op jit(solution)/shard_map/all_gather | solution.py:119
  9.6 214.2 %all-reduce.6.cloned.1.call-start = ((), (), s32[]{:S(2)}) async-start(), calls=%async_computation.2 | async-start | bytes 8388608
  69.1 3.4 copy-start.2
  72.5 2.1 copy-start
  72.5 4.1 %copy-start.11 = (bf16[4096,462]{0,1:T(8,128)(2,1)S(1)}, bf16[4096,462]{0,1:T(8,128)(2,1)}, u32[]{:S(2)}) copy-start(bf16[4096,462]{0,1:T(8,128)(2,1)} %param.15) | copy-start | bytes 11354116
  73.7 4.1 %copy-start.10 = (bf16[4096,462]{0,1:T(8,128)(2,1)S(1)}, bf16[4096,462]{0,1:T(8,128)(2,1)}, u32[]{:S(2)}) copy-start(bf16[4096,462]{0,1:T(8,128)(2,1)} %param.16) | copy-start | bytes 11354116
  77.8 2.1 copy-start.3
  79.9 2.2 copy-start.7
  80.0 143.9 %copy-start.4 = (bf16[4,4096]{1,0:T(4,128)(2,1)S(1)}, bf16[4,4096]{1,0:T(4,128)(2,1)}, u32[]{:S(2)}) copy-start(bf16[4,4096]{1,0:T(4,128)(2,1)} %param.12) | copy-start | bytes 98308
  80.0 144.9 %copy-start.5 = (s32[4]{0:T(128)S(1)}, s32[4]{0:T(128)}, u32[]{:S(2)}) copy-start(s32[4]{0:T(128)} %param.13) | copy-start | bytes 52
  82.1 185.1 %copy-start.8 = (f32[1,32]{1,0:T(1,128)S(1)}, f32[1,32]{1,0:T(1,128)}, u32[]{:S(2)}) copy-start(f32[1,32]{1,0:T(1,128)} %param.23) | copy-start | bytes 388
  82.1 185.2 %copy-start.6 = (s32[1,32]{1,0:T(1,128)S(1)}, s32[1,32]{1,0:T(1,128)}, u32[]{:S(2)}) copy-start(s32[1,32]{1,0:T(1,128)} %param.22) | copy-start | bytes 388
  82.1 240.3 %all-gather.8.cloned.1.call-start = ((), (), s32[]{:S(2)}) async-start(), calls=%async_computation.1 | async-start | bytes 1081344 | tf_op jit(solution)/shard_map/all_gather | solution.py:152
  267.4 60.6 %copy-start.9 = (f32[1,32]{1,0:T(1,128)}, f32[1,32]{1,0:T(1,128)S(1)}, u32[]{:S(2)}) copy-start(f32[1,32]{1,0:T(1,128)S(1)} %fusion.20) | copy-start | bytes 388
  323.8 4.3 %copy-start.1 = (bf16[462,4096]{1,0:T(8,128)(2,1)S(1)}, bf16[462,4096]{1,0:T(8,128)(2,1)}, u32[]{:S(2)}) copy-start(bf16[462,4096]{1,0:T(8,128)(2,1)} %param.20) | copy-start | bytes 11354116
Sparse Core Ops, SparseCore 0:
  11.4 56.3 all-gather.5
  82.2 141.5 all-reduce.5
  269.3 53.0 all-gather.7
